TPU v7x, 256 devices: a whole 4x4x8 slice. The times are simulated.
256 devices in a mesh: tile: 128 (over z_hi, x, y, core), member: 2 (over z_lo).
Axes of the slice: x: 4, y: 4, z: 8 (z_hi: 4, z_lo: 2; z = z_hi * 2 + z_lo), core: 2. Of those that a mesh axis runs over, the one named last changes fastest.
Arguments:
- fields: bfloat16 [2, 128, 2, 32, 32, 128], P('member', 'tile'), may hold values from -6 to 6
- cotangent: bfloat16 [2, 128, 2, 32, 32, 128], P('member', 'tile'), may hold values from -6 to 6
- edge_map: int32 [128, 4, 2], P('tile'), may hold values from 0 to 3, as said below
- w_first: bfloat16 [3, 3, 128, 128], replicated, may hold values from -0.1875 to 0.1875
- b_first: float32 [128], replicated, may hold values from -3 to 3
- w_second: bfloat16 [3, 3, 128, 128], replicated, may hold values from -0.1875 to 0.1875
- b_second: float32 [128], replicated, may hold values from -3 to 3
Outputs:
- response: bfloat16 [2, 128, 2, 32, 32, 128], P('member', 'tile')
- field_grad: bfloat16 [2, 128, 2, 32, 32, 128], P('member', 'tile')
- first_kernel_grad: float32 [3, 3, 128, 128], replicated
- first_bias_grad: float32 [128], replicated
- second_kernel_grad: float32 [3, 3, 128, 128], replicated
- second_bias_grad: float32 [128], replicated
Inputs may be any that keep to these rules, and one draw needn't show every extreme that they name: Each tile t is its own grid turned by r quarter turns: edge_map[t, g, 0] = (g - r) mod 4, and edge_map[t, g, 1] is 1 exactly when r = 2, or r = 1 and g is even, or r = 3 and g is odd.
All inputs are finite; a program needn't handle non-finite values.
Results may differ from a plain program's by a relative error of at most 0.0065.
Values may be sent and summed in bfloat16 or wider, within the bound.
A program may use at most 64 MiB of HBM per device.

v0:
```python
import jax
import jax.numpy as jnp
from jax import lax
from jax.sharding import PartitionSpec as P

ROW_TILES = 8
ROOT_HALF = 0.7071067811865476
INV_ROOT_TAU = 0.3989422804014327


def shifted(value, axis, steps):
    count = lax.axis_size(axis)
    pairs = [(source, (source + steps) % count) for source in range(count)]
    return lax.ppermute(value, axis, pairs)


def gelu_value(inputs):
    return 0.5 * inputs * (1.0 + jax.scipy.special.erf(inputs * ROOT_HALF))


def gelu_slope(inputs):
    return (
        0.5 * (1.0 + jax.scipy.special.erf(inputs * ROOT_HALF))
        + inputs * jnp.exp(-0.5 * inputs * inputs) * INV_ROOT_TAU
    )


def patches(padded):
    out_rows = padded.shape[-3] - 2
    out_cols = padded.shape[-2] - 2
    pieces = [
        padded[..., row_off : row_off + out_rows, col_off : col_off + out_cols, :]
        for row_off in range(3)
        for col_off in range(3)
    ]
    joined = jnp.concatenate(pieces, axis=-1)
    return joined.reshape(-1, joined.shape[-1])


def rim_strips(tile_data):
    return jnp.stack(
        [
            tile_data[..., 0, :, :],
            tile_data[..., :, -1, :],
            tile_data[..., -1, :, :],
            tile_data[..., :, 0, :],
        ],
        axis=-4,
    )


def orient(strips, chosen_ids, flip_ids):
    shaped_ids = chosen_ids.reshape(chosen_ids.shape + (1, 1, 1))
    shaped_flips = flip_ids.reshape(flip_ids.shape + (1, 1, 1))
    chosen = jnp.zeros_like(strips)
    for candidate in range(4):
        chosen = jnp.where(
            shaped_ids == candidate, jnp.expand_dims(strips[..., candidate, :, :, :], -4), chosen
        )
    flipped = chosen[..., ::-1, :]
    return jnp.where(shaped_flips == 1, flipped, chosen)


def assemble(tile_data, placed):
    top_rim = placed[..., 0, :, :, :]
    right_rim = placed[..., 1, :, :, :]
    bottom_rim = placed[..., 2, :, :, :]
    left_rim = placed[..., 3, :, :, :]
    kind = tile_data.dtype
    top_left = (
        0.5 * (top_rim[..., 0, :].astype(jnp.float32) + left_rim[..., 0, :].astype(jnp.float32))
    ).astype(kind)
    top_right = (
        0.5 * (top_rim[..., -1, :].astype(jnp.float32) + right_rim[..., 0, :].astype(jnp.float32))
    ).astype(kind)
    low_left = (
        0.5 * (bottom_rim[..., 0, :].astype(jnp.float32) + left_rim[..., -1, :].astype(jnp.float32))
    ).astype(kind)
    low_right = (
        0.5
        * (bottom_rim[..., -1, :].astype(jnp.float32) + right_rim[..., -1, :].astype(jnp.float32))
    ).astype(kind)
    top_row = jnp.concatenate([top_left[..., None, :], top_rim, top_right[..., None, :]], axis=-2)
    bottom_row = jnp.concatenate(
        [low_left[..., None, :], bottom_rim, low_right[..., None, :]], axis=-2
    )
    middle = jnp.concatenate(
        [left_rim[..., :, None, :], tile_data, right_rim[..., :, None, :]], axis=-2
    )
    return jnp.concatenate([top_row[..., None, :, :], middle, bottom_row[..., None, :, :]], axis=-3)


def fold_rims(grad_pad):
    interior = grad_pad[..., 1:-1, 1:-1, :]
    top_left = 0.5 * grad_pad[..., 0, 0, :]
    top_right = 0.5 * grad_pad[..., 0, -1, :]
    low_left = 0.5 * grad_pad[..., -1, 0, :]
    low_right = 0.5 * grad_pad[..., -1, -1, :]
    top_rim = grad_pad[..., 0, 1:-1, :].at[..., 0, :].add(top_left).at[..., -1, :].add(top_right)
    right_rim = (
        grad_pad[..., 1:-1, -1, :].at[..., 0, :].add(top_right).at[..., -1, :].add(low_right)
    )
    bottom_rim = (
        grad_pad[..., -1, 1:-1, :].at[..., 0, :].add(low_left).at[..., -1, :].add(low_right)
    )
    left_rim = grad_pad[..., 1:-1, 0, :].at[..., 0, :].add(top_left).at[..., -1, :].add(low_left)
    return (interior, jnp.stack([top_rim, right_rim, bottom_rim, left_rim], axis=-4))


def spread(interior, edge_grads):
    interior = interior.at[..., 0, :, :].add(edge_grads[..., 0, :, :, :])
    interior = interior.at[..., :, -1, :].add(edge_grads[..., 1, :, :, :])
    interior = interior.at[..., -1, :, :].add(edge_grads[..., 2, :, :, :])
    return interior.at[..., :, 0, :].add(edge_grads[..., 3, :, :, :])


def trade_rims(outgoing):
    offsets = (ROW_TILES, -1, -ROW_TILES, 1)
    received = []
    for direction in range(4):
        received.append(shifted(outgoing[(direction + 2) % 4], "tile", offsets[direction]))
    return jnp.stack(received)


def trade_grads(outgoing):
    offsets = (ROW_TILES, -1, -ROW_TILES, 1)
    received = []
    for direction in range(4):
        received.append(
            shifted(
                outgoing[(direction + 2) % 4].astype(jnp.bfloat16), "tile", offsets[direction]
            ).astype(jnp.float32)
        )
    return jnp.stack(received)


def pad_tile(tile_data, tables):
    side_ids, flip_marks, inverse, inverse_marks = tables
    outgoing = orient(rim_strips(tile_data), side_ids, flip_marks)
    incoming = trade_rims(outgoing)
    return assemble(tile_data, orient(incoming, inverse, inverse_marks))


def unpad_tile(grad_pad, tables):
    side_ids, flip_marks, inverse, inverse_marks = tables
    interior, placed = fold_rims(grad_pad)
    outgoing = orient(placed, side_ids, flip_marks)
    incoming = trade_grads(outgoing)
    return spread(interior, orient(incoming, inverse, inverse_marks))


def apply_cat(padded, weights_cat, out_rows, out_cols):
    product = jnp.dot(patches(padded), weights_cat, preferred_element_type=jnp.float32)
    return product.reshape(padded.shape[0], out_rows, out_cols, -1)


def forward_conv(tile_data, weights_cat, tables):
    tile_side = tile_data.shape[1]
    padded = pad_tile(tile_data, tables)
    result = apply_cat(padded, weights_cat, tile_side, tile_side)
    return (result, padded)


def back_conv(grad_data, weights_flip):
    tile_side = grad_data.shape[1]
    zero_pad = jnp.pad(grad_data, ((0, 0), (2, 2), (2, 2), (0, 0)))
    return apply_cat(zero_pad, weights_flip, tile_side + 2, tile_side + 2)


def kernel_term(padded, grad_data):
    channels = grad_data.shape[-1]
    total = lax.dot_general(
        patches(padded),
        grad_data.reshape(-1, channels),
        (((0,), (0,)), ((), ())),
        preferred_element_type=jnp.float32,
    )
    return total.reshape(3, 3, channels, channels)


def per_device(fields, cotangent, edge_map, w_first, b_first, w_second, b_second):
    frames, tile_side, channels = (fields.shape[2], fields.shape[3], fields.shape[5])
    source = fields.reshape(fields.shape[2:])
    upstream = cotangent.reshape(cotangent.shape[2:])
    side_ids = edge_map[0, :, 0]
    flip_marks = edge_map[0, :, 1]
    directions = jnp.arange(4, dtype=jnp.int32)
    inverse = jnp.sum(directions[None, :] * (side_ids[None, :] == directions[:, None]), axis=1)
    inverse_marks = jnp.take(flip_marks, inverse)
    tables = (side_ids, flip_marks, inverse, inverse_marks)
    first_cat = w_first.reshape(9 * channels, channels)
    second_cat = w_second.reshape(9 * channels, channels)
    first_flip = w_first[::-1, ::-1].transpose(0, 1, 3, 2).reshape(9 * channels, channels)
    second_flip = w_second[::-1, ::-1].transpose(0, 1, 3, 2).reshape(9 * channels, channels)
    norm_scale = float(
        lax.axis_size("tile") * lax.axis_size("member") * frames * tile_side * tile_side
    ) ** (-0.5)
    pre_one, pad_first = forward_conv(source, first_cat, tables)
    hidden_one = pre_one + b_first
    activity = gelu_value(hidden_one).astype(jnp.bfloat16)
    pre_two, pad_second = forward_conv(activity, second_cat, tables)
    hidden_two = pre_two + b_second
    response = gelu_value(hidden_two).astype(jnp.bfloat16)
    grad_second = (upstream.astype(jnp.float32) * gelu_slope(hidden_two)).astype(jnp.bfloat16)
    kernel_two = kernel_term(pad_second, grad_second)
    bias_two = jnp.sum(grad_second.astype(jnp.float32), axis=(0, 1, 2))
    grad_act = unpad_tile(back_conv(grad_second, second_flip), tables)
    grad_first = (grad_act * gelu_slope(hidden_one)).astype(jnp.bfloat16)
    kernel_one = kernel_term(pad_first, grad_first)
    bias_one = jnp.sum(grad_first.astype(jnp.float32), axis=(0, 1, 2))
    field_grad = unpad_tile(back_conv(grad_first, first_flip), tables).astype(jnp.bfloat16)
    kernel_one, bias_one, kernel_two, bias_two = lax.psum(
        (kernel_one, bias_one, kernel_two, bias_two), ("tile", "member")
    )
    return (
        response.reshape(fields.shape),
        field_grad.reshape(fields.shape),
        kernel_one * norm_scale,
        bias_one * norm_scale,
        kernel_two * norm_scale,
        bias_two * norm_scale,
    )


def solution(mesh):
    in_specs = (
        P("member", "tile", None, None, None, None),
        P("member", "tile", None, None, None, None),
        P("tile", None, None),
        P(),
        P(),
        P(),
        P(),
    )
    out_specs = (
        P("member", "tile", None, None, None, None),
        P("member", "tile", None, None, None, None),
        P(),
        P(),
        P(),
        P(),
    )
    return jax.shard_map(
        per_device, mesh=mesh, in_specs=in_specs, out_specs=out_specs, check_vma=False
    )
```

profile of v0, /device:TPU:2, one launch (start us, length us, event | category | flops | bytes accessed | tf_op | source)
XLA Modules:
  0.0 479.1 jit_solution(9307611065890658141)
XLA Ops:
  10.2 1.6 collective-permute-start.3
  11.8 3.5 collective-permute-start.2
  15.3 6.0 %collective-permute-start.1 = (bf16[2,32,128]{2,1,0:T(8,128)(2,1)S(1)}, bf16[2,32,128]{2,1,0:T(8,128)(2,1)S(1)}, u32[]{:S(2)}, u32[]{:S(2)}) collective-permute-start(bf16[2,32,128]{2,1,0:T(8,128)(2,1)S(1)} %get-tuple-element.401), channel_id=1, source_target_pairs={{0,240},{2,242},{4,244},{6,246},{8,248},{10,250},{12,252},{14,254}... | collective-permute-start | bytes 49160 | tf_op jit(solution)/shard_map/ppermute | solution.py:14
  22.9 1.2 copy.158
  24.8 1.2 copy.140
  30.4 1.1 constant_dynamic-update-slice_fusion.3
  31.5 1.5 fusion.78
  33.5 1.4 fusion.84
  36.3 3.8 collective-permute-start.6
  40.0 6.2 %collective-permute-start.5 = (bf16[2,32,128]{2,1,0:T(8,128)(2,1)S(1)}, bf16[2,32,128]{2,1,0:T(8,128)(2,1)S(1)}, u32[]{:S(2)}, u32[]{:S(2)}) collective-permute-start(bf16[2,32,128]{2,1,0:T(8,128)(2,1)S(1)} %get-tuple-element.391), channel_id=1, source_target_pairs={{0,240},{2,242},{4,244},{6,246},{8,248},{10,250},{12,252},{14,254}... | collective-permute-start | bytes 49160 | tf_op jit(solution)/shard_map/ppermute | solution.py:14
  46.2 1.9 constant_dynamic-update-slice_fusion.18
  50.0 1.9 constant_dynamic-update-slice_fusion.15
  56.3 6.7 %copy.180 = bf16[1152,2048]{1,0:T(8,128)(2,1)} copy(bf16[1152,2048]{0,1:T(8,128)(2,1)} %bitcast.102) | data formatting | bytes 9437184 | tf_op jit(solution)/shard_map/dot_general | solution.py:172
  66.4 4.8 %copy.182 = bf16[2,32,32,1152]{3,2,1,0:T(8,128)(2,1)} copy(bf16[2,32,32,1152]{3,1,0,2:T(8,128)(2,1)S(1)} %slice_dynamic-update-slice_fusion) | data formatting | bytes 9437184 | tf_op jit(solution)/shard_map/concatenate | solution.py:36
  71.3 2.5 convert_reduce_fusion
  76.5 2.3 fusion.2
  80.7 6.7 %copy.183 = bf16[1152,2048]{1,0:T(8,128)(2,1)} copy(bf16[1152,2048]{0,1:T(8,128)(2,1)} %bitcast.263) | data formatting | bytes 9437184 | tf_op jit(solution)/shard_map/dot_general | solution.py:172
  93.7 1.4 select_select_fusion.3
  97.1 3.8 collective-permute-start.10
  100.8 6.0 %collective-permute-start.9 = (bf16[2,32,128]{2,1,0:T(8,128)(2,1)S(1)}, bf16[2,32,128]{2,1,0:T(8,128)(2,1)S(1)}, u32[]{:S(2)}, u32[]{:S(2)}) collective-permute-start(bf16[2,32,128]{2,1,0:T(8,128)(2,1)S(1)} %get-tuple-element.381), channel_id=1, source_target_pairs={{0,240},{2,242},{4,244},{6,246},{8,248},{10,250},{12,252},{14,254}... | collective-permute-start | bytes 49160 | tf_op jit(solution)/shard_map/ppermute | solution.py:14
  106.9 4.6 fusion.86
  111.6 1.1 copy.185
  117.4 2.1 fusion
  119.7 73.3 %all-reduce.2 = (f32[128]{0:T(128)S(1)}, f32[128]{0:T(128)S(1)}) all-reduce(f32[128]{0:T(128)S(1)} %get-tuple-element.318, f32[128]{0:T(128)S(1)} %copy-done.40), channel_id=1, replica_groups=mesh['tile'=128,'member'=2] {'tile','member'}, use_global_device_ids=true, to_apply=%region_3.4 | all-reduce | flops 256 | bytes 2048 | tf_op jit(solution)/shard_map/psum | solution.py:212
  194.1 2.3 collective-permute-start.15
  196.4 3.5 collective-permute-start.14
  199.9 5.4 %collective-permute-start.13 = (bf16[2,32,128]{2,1,0:T(8,128)(2,1)S(1)}, bf16[2,32,128]{2,1,0:T(8,128)(2,1)S(1)}, u32[]{:S(2)}, u32[]{:S(2)}) collective-permute-start(bf16[2,32,128]{2,1,0:T(8,128)(2,1)S(1)} %get-tuple-element.377), channel_id=1, source_target_pairs={{0,240},{2,242},{4,244},{6,246},{8,248},{10,250},{12,252},{14,254}... | collective-permute-start | bytes 49160 | tf_op jit(solution)/shard_map/ppermute | solution.py:14
  205.3 4.5 fusion.85
  211.7 1.1 copy.186
  212.8 255.2 %all-reduce.6.cloned.1.call-done = (f32[3,3,128,128]{3,2,1,0:T(8,128)}, f32[3,3,128,128]{3,2,1,0:T(8,128)}) async-done(((f32[3,3,128,128]{3,2,1,0:T(8,128)}, f32[3,3,128,128]{3,2,1,0:T(8,128)}), (f32[3,3,128,128]{3,2,1,0:T(8,128)}, f32[3,3,128,128]{3,2,1,0:T(8,128)})) %all-reduce.6.cloned.1.call-update) | async-done | bytes 1179664 | tf_op jit(solution)/shard_map/psum | solution.py:212
  468.0 1.9 broadcast_multiply_fusion.1
  469.9 1.9 broadcast_multiply_fusion
  (273 shorter events, 40.7 us)
Async XLA Ops:
  7.2 460.8 %all-reduce.6.cloned.1.call-start = ((), (), s32[]{:S(2)}) async-start(), calls=%async_computation | async-start | bytes 2359296 | tf_op jit(solution)/shard_map/psum | solution.py:212
  9.8 26.1 %copy-start.24 = (pred[4]{0:T(512)(128)(4,1)}, pred[4]{0:T(512)(128)(4,1)S(1)}, u32[]{:S(2)}) copy-start(pred[4]{0:T(512)(128)(4,1)S(1)} %get-tuple-element.428) | copy-start | bytes 16
  9.8 26.1 %copy-start.26 = (pred[4]{0:T(512)(128)(4,1)}, pred[4]{0:T(512)(128)(4,1)S(1)}, u32[]{:S(2)}) copy-start(pred[4]{0:T(512)(128)(4,1)S(1)} %get-tuple-element.429) | copy-start | bytes 16
  9.8 26.1 %copy-start.28 = (pred[4]{0:T(512)(128)(4,1)}, pred[4]{0:T(512)(128)(4,1)S(1)}, u32[]{:S(2)}) copy-start(pred[4]{0:T(512)(128)(4,1)S(1)} %get-tuple-element.430) | copy-start | bytes 16
  9.8 26.1 %copy-start.32 = (pred[4]{0:T(512)(128)(4,1)}, pred[4]{0:T(512)(128)(4,1)S(1)}, u32[]{:S(2)}) copy-start(pred[4]{0:T(512)(128)(4,1)S(1)} %get-tuple-element.426) | copy-start | bytes 16
  10.1 16.6 %collective-permute-start = (bf16[2,32,128]{2,1,0:T(8,128)(2,1)S(1)}, bf16[2,32,128]{2,1,0:T(8,128)(2,1)S(1)}, u32[]{:S(2)}, u32[]{:S(2)}) collective-permute-start(bf16[2,32,128]{2,1,0:T(8,128)(2,1)S(1)} %get-tuple-element.398), channel_id=1, source_target_pairs={{0,2},{2,4},{4,6},{6,8},{8,10},{10,12},{12,14},{14,16},{16,18},{18... | collective-permute-start | bytes 49160 | tf_op jit(solution)/shard_map/ppermute | solution.py:14
  10.2 16.5 %collective-permute-start.3 = (bf16[2,32,128]{2,1,0:T(8,128)(2,1)S(1)}, bf16[2,32,128]{2,1,0:T(8,128)(2,1)S(1)}, u32[]{:S(2)}, u32[]{:S(2)}) collective-permute-start(bf16[2,32,128]{2,1,0:T(8,128)(2,1)S(1)} %get-tuple-element.399), channel_id=1, source_target_pairs={{0,16},{2,18},{4,20},{6,22},{8,24},{10,26},{12,28},{14,30},{16,32}... | collective-permute-start | bytes 49160 | tf_op jit(solution)/shard_map/ppermute | solution.py:14
  11.8 15.0 %collective-permute-start.2 = (bf16[2,32,128]{2,1,0:T(8,128)(2,1)S(1)}, bf16[2,32,128]{2,1,0:T(8,128)(2,1)S(1)}, u32[]{:S(2)}, u32[]{:S(2)}) collective-permute-start(bf16[2,32,128]{2,1,0:T(8,128)(2,1)S(1)} %get-tuple-element.400), channel_id=1, source_target_pairs={{0,254},{2,0},{4,2},{6,4},{8,6},{10,8},{12,10},{14,12},{16,14},{18... | collective-permute-start | bytes 49160 | tf_op jit(solution)/shard_map/ppermute | solution.py:14
  15.3 11.5 %collective-permute-start.1 = (bf16[2,32,128]{2,1,0:T(8,128)(2,1)S(1)}, bf16[2,32,128]{2,1,0:T(8,128)(2,1)S(1)}, u32[]{:S(2)}, u32[]{:S(2)}) collective-permute-start(bf16[2,32,128]{2,1,0:T(8,128)(2,1)S(1)} %get-tuple-element.401), channel_id=1, source_target_pairs={{0,240},{2,242},{4,244},{6,246},{8,248},{10,250},{12,252},{14,254}... | collective-permute-start | bytes 49160 | tf_op jit(solution)/shard_map/ppermute | solution.py:14
  22.8 40.4 %copy-start.14 = (pred[4]{0:T(512)(128)(4,1)}, pred[4]{0:T(512)(128)(4,1)S(1)}, u32[]{:S(2)}) copy-start(pred[4]{0:T(512)(128)(4,1)S(1)} %get-tuple-element.432) | copy-start | bytes 16
  22.8 40.4 %copy-start.16 = (pred[4]{0:T(512)(128)(4,1)}, pred[4]{0:T(512)(128)(4,1)S(1)}, u32[]{:S(2)}) copy-start(pred[4]{0:T(512)(128)(4,1)S(1)} %get-tuple-element.433) | copy-start | bytes 16
  22.9 40.4 %copy-start.18 = (pred[4]{0:T(512)(128)(4,1)}, pred[4]{0:T(512)(128)(4,1)S(1)}, u32[]{:S(2)}) copy-start(pred[4]{0:T(512)(128)(4,1)S(1)} %get-tuple-element.434) | copy-start | bytes 16
  22.9 40.4 %copy-start.20 = (pred[4]{0:T(512)(128)(4,1)}, pred[4]{0:T(512)(128)(4,1)S(1)}, u32[]{:S(2)}) copy-start(pred[4]{0:T(512)(128)(4,1)S(1)} %get-tuple-element.435) | copy-start | bytes 16
  22.9 40.4 %copy-start.30 = (pred[4]{0:T(512)(128)(4,1)}, pred[4]{0:T(512)(128)(4,1)S(1)}, u32[]{:S(2)}) copy-start(pred[4]{0:T(512)(128)(4,1)S(1)} %get-tuple-element.431) | copy-start | bytes 16
  36.1 27.0 %collective-permute-start.4 = (bf16[2,32,128]{2,1,0:T(8,128)(2,1)S(1)}, bf16[2,32,128]{2,1,0:T(8,128)(2,1)S(1)}, u32[]{:S(2)}, u32[]{:S(2)}) collective-permute-start(bf16[2,32,128]{2,1,0:T(8,128)(2,1)S(1)} %get-tuple-element.388), channel_id=1, source_target_pairs={{0,2},{2,4},{4,6},{6,8},{8,10},{10,12},{12,14},{14,16},{16,18},{18... | collective-permute-start | bytes 49160 | tf_op jit(solution)/shard_map/ppermute | solution.py:14
  36.2 26.9 %collective-permute-start.7 = (bf16[2,32,128]{2,1,0:T(8,128)(2,1)S(1)}, bf16[2,32,128]{2,1,0:T(8,128)(2,1)S(1)}, u32[]{:S(2)}, u32[]{:S(2)}) collective-permute-start(bf16[2,32,128]{2,1,0:T(8,128)(2,1)S(1)} %get-tuple-element.389), channel_id=1, source_target_pairs={{0,16},{2,18},{4,20},{6,22},{8,24},{10,26},{12,28},{14,30},{16,32}... | collective-permute-start | bytes 49160 | tf_op jit(solution)/shard_map/ppermute | solution.py:14
  36.3 26.8 %collective-permute-start.6 = (bf16[2,32,128]{2,1,0:T(8,128)(2,1)S(1)}, bf16[2,32,128]{2,1,0:T(8,128)(2,1)S(1)}, u32[]{:S(2)}, u32[]{:S(2)}) collective-permute-start(bf16[2,32,128]{2,1,0:T(8,128)(2,1)S(1)} %get-tuple-element.390), channel_id=1, source_target_pairs={{0,254},{2,0},{4,2},{6,4},{8,6},{10,8},{12,10},{14,12},{16,14},{18... | collective-permute-start | bytes 49160 | tf_op jit(solution)/shard_map/ppermute | solution.py:14
  40.0 23.0 %collective-permute-start.5 = (bf16[2,32,128]{2,1,0:T(8,128)(2,1)S(1)}, bf16[2,32,128]{2,1,0:T(8,128)(2,1)S(1)}, u32[]{:S(2)}, u32[]{:S(2)}) collective-permute-start(bf16[2,32,128]{2,1,0:T(8,128)(2,1)S(1)} %get-tuple-element.391), channel_id=1, source_target_pairs={{0,240},{2,242},{4,244},{6,246},{8,248},{10,250},{12,252},{14,254}... | collective-permute-start | bytes 49160 | tf_op jit(solution)/shard_map/ppermute | solution.py:14
  96.9 15.9 %collective-permute-start.8 = (bf16[2,32,128]{2,1,0:T(8,128)(2,1)S(1)}, bf16[2,32,128]{2,1,0:T(8,128)(2,1)S(1)}, u32[]{:S(2)}, u32[]{:S(2)}) collective-permute-start(bf16[2,32,128]{2,1,0:T(8,128)(2,1)S(1)} %get-tuple-element.378), channel_id=1, source_target_pairs={{0,2},{2,4},{4,6},{6,8},{8,10},{10,12},{12,14},{14,16},{16,18},{18... | collective-permute-start | bytes 49160 | tf_op jit(solution)/shard_map/ppermute | solution.py:14
  97.0 15.8 %collective-permute-start.11 = (bf16[2,32,128]{2,1,0:T(8,128)(2,1)S(1)}, bf16[2,32,128]{2,1,0:T(8,128)(2,1)S(1)}, u32[]{:S(2)}, u32[]{:S(2)}) collective-permute-start(bf16[2,32,128]{2,1,0:T(8,128)(2,1)S(1)} %get-tuple-element.379), channel_id=1, source_target_pairs={{0,16},{2,18},{4,20},{6,22},{8,24},{10,26},{12,28},{14,30},{16,32}... | collective-permute-start | bytes 49160 | tf_op jit(solution)/shard_map/ppermute | solution.py:14
  97.1 15.8 %collective-permute-start.10 = (bf16[2,32,128]{2,1,0:T(8,128)(2,1)S(1)}, bf16[2,32,128]{2,1,0:T(8,128)(2,1)S(1)}, u32[]{:S(2)}, u32[]{:S(2)}) collective-permute-start(bf16[2,32,128]{2,1,0:T(8,128)(2,1)S(1)} %get-tuple-element.380), channel_id=1, source_target_pairs={{0,254},{2,0},{4,2},{6,4},{8,6},{10,8},{12,10},{14,12},{16,14},{18... | collective-permute-start | bytes 49160 | tf_op jit(solution)/shard_map/ppermute | solution.py:14
  100.8 12.0 %collective-permute-start.9 = (bf16[2,32,128]{2,1,0:T(8,128)(2,1)S(1)}, bf16[2,32,128]{2,1,0:T(8,128)(2,1)S(1)}, u32[]{:S(2)}, u32[]{:S(2)}) collective-permute-start(bf16[2,32,128]{2,1,0:T(8,128)(2,1)S(1)} %get-tuple-element.381), channel_id=1, source_target_pairs={{0,240},{2,242},{4,244},{6,246},{8,248},{10,250},{12,252},{14,254}... | collective-permute-start | bytes 49160 | tf_op jit(solution)/shard_map/ppermute | solution.py:14
  117.4 76.2 %copy-start.35 = (f32[2,1,1,128]{3,1,2,0:T(1,128)S(1)}, f32[2,1,1,128]{3,1,2,0:T(1,128)}, u32[]{:S(2)}) copy-start(f32[2,1,1,128]{3,1,2,0:T(1,128)} %copy-done.34) | copy-start | bytes 3076
  117.4 76.3 %copy-start.23 = (pred[4]{0:T(512)(128)(4,1)S(1)}, pred[4]{0:T(512)(128)(4,1)}, u32[]{:S(2)}) copy-start(pred[4]{0:T(512)(128)(4,1)} %copy-done.22) | copy-start | bytes 16
  117.4 76.3 %copy-start.25 = (pred[4]{0:T(512)(128)(4,1)S(1)}, pred[4]{0:T(512)(128)(4,1)}, u32[]{:S(2)}) copy-start(pred[4]{0:T(512)(128)(4,1)} %copy-done.24) | copy-start | bytes 16
  117.4 76.3 %copy-start.27 = (pred[4]{0:T(512)(128)(4,1)S(1)}, pred[4]{0:T(512)(128)(4,1)}, u32[]{:S(2)}) copy-start(pred[4]{0:T(512)(128)(4,1)} %copy-done.26) | copy-start | bytes 16
  117.4 76.3 %copy-start.29 = (pred[4]{0:T(512)(128)(4,1)S(1)}, pred[4]{0:T(512)(128)(4,1)}, u32[]{:S(2)}) copy-start(pred[4]{0:T(512)(128)(4,1)} %copy-done.28) | copy-start | bytes 16
  117.4 76.5 %copy-start.33 = (pred[4]{0:T(512)(128)(4,1)S(1)}, pred[4]{0:T(512)(128)(4,1)}, u32[]{:S(2)}) copy-start(pred[4]{0:T(512)(128)(4,1)} %copy-done.32) | copy-start | bytes 16
  194.0 16.6 %collective-permute-start.12 = (bf16[2,32,128]{2,1,0:T(8,128)(2,1)S(1)}, bf16[2,32,128]{2,1,0:T(8,128)(2,1)S(1)}, u32[]{:S(2)}, u32[]{:S(2)}) collective-permute-start(bf16[2,32,128]{2,1,0:T(8,128)(2,1)S(1)} %get-tuple-element.374), channel_id=1, source_target_pairs={{0,2},{2,4},{4,6},{6,8},{8,10},{10,12},{12,14},{14,16},{16,18},{18... | collective-permute-start | bytes 49160 | tf_op jit(solution)/shard_map/ppermute | solution.py:14
  194.1 16.6 %collective-permute-start.15 = (bf16[2,32,128]{2,1,0:T(8,128)(2,1)S(1)}, bf16[2,32,128]{2,1,0:T(8,128)(2,1)S(1)}, u32[]{:S(2)}, u32[]{:S(2)}) collective-permute-start(bf16[2,32,128]{2,1,0:T(8,128)(2,1)S(1)} %get-tuple-element.375), channel_id=1, source_target_pairs={{0,16},{2,18},{4,20},{6,22},{8,24},{10,26},{12,28},{14,30},{16,32}... | collective-permute-start | bytes 49160 | tf_op jit(solution)/shard_map/ppermute | solution.py:14
  196.4 14.3 %collective-permute-start.14 = (bf16[2,32,128]{2,1,0:T(8,128)(2,1)S(1)}, bf16[2,32,128]{2,1,0:T(8,128)(2,1)S(1)}, u32[]{:S(2)}, u32[]{:S(2)}) collective-permute-start(bf16[2,32,128]{2,1,0:T(8,128)(2,1)S(1)} %get-tuple-element.376), channel_id=1, source_target_pairs={{0,254},{2,0},{4,2},{6,4},{8,6},{10,8},{12,10},{14,12},{16,14},{18... | collective-permute-start | bytes 49160 | tf_op jit(solution)/shard_map/ppermute | solution.py:14
  199.9 10.8 %collective-permute-start.13 = (bf16[2,32,128]{2,1,0:T(8,128)(2,1)S(1)}, bf16[2,32,128]{2,1,0:T(8,128)(2,1)S(1)}, u32[]{:S(2)}, u32[]{:S(2)}) collective-permute-start(bf16[2,32,128]{2,1,0:T(8,128)(2,1)S(1)} %get-tuple-element.377), channel_id=1, source_target_pairs={{0,240},{2,242},{4,244},{6,246},{8,248},{10,250},{12,252},{14,254}... | collective-permute-start | bytes 49160 | tf_op jit(solution)/shard_map/ppermute | solution.py:14
  (26 other events, 185.3 us)
Sparse Core Ops, SparseCore 0:
  210.8 257.1 all-reduce.5
where the time goes:
time: 489 us; the launch traced here: 479 us
  waiting for transfers between devices  255 us (52%)
  blocking collectives  73.3 us (15%)
  local copies, waits for them, and re-layouts  56.4 us (12%)
  starting transfers between devices  42.5 us (9%)
  other arithmetic  18.3 us (4%)
  matrix products  17.4 us (4%)
  between operations  15.9 us (3%)
    psum x1, waiting for transfers between devices, per_device(): lax.psum((kernel_one, bias_one, kernel_two, bias_two), ('tile', 'member'))  255 us
    psum x1, blocking collectives, per_device(): lax.psum((kernel_one, bias_one, kernel_two, bias_two), ('tile', 'member'))  73.3 us
    ppermute x16, starting transfers between devices, shifted(): return lax.ppermute(value, axis, pairs)  42.5 us
    unnamed x134, local copies, waits for them, and re-layouts  23.3 us
    dot_general x2, local copies, waits for them, and re-layouts, kernel_term(): lax.dot_general(patches(padded), grad_data.reshape(-1, channels), (((0,),...  13.4 us
  transfers between devices with their start and end apart: 17, of which 1 were waited for; matrix products, arithmetic and copies ran while one was open for 7% of the time, Pallas kernels for 0%

commit v1 on v0

--- a/solution.py
+++ b/solution.py
@@ -2,6 +2,7 @@
 import jax.numpy as jnp
 from jax import lax
 from jax.sharding import PartitionSpec as P
+from jax.lax import psum
 
 ROW_TILES = 8
 ROOT_HALF = 0.7071067811865476
@@ -179,6 +180,10 @@
 
 
 def per_device(fields, cotangent, edge_map, w_first, b_first, w_second, b_second):
+
+    def perform_the_files(arr):
+        return psum(psum(arr, "member"), "tile")
+
     frames, tile_side, channels = (fields.shape[2], fields.shape[3], fields.shape[5])
     source = fields.reshape(fields.shape[2:])
     upstream = cotangent.reshape(cotangent.shape[2:])
@@ -209,8 +214,8 @@
     kernel_one = kernel_term(pad_first, grad_first)
     bias_one = jnp.sum(grad_first.astype(jnp.float32), axis=(0, 1, 2))
     field_grad = unpad_tile(back_conv(grad_first, first_flip), tables).astype(jnp.bfloat16)
-    kernel_one, bias_one, kernel_two, bias_two = lax.psum(
-        (kernel_one, bias_one, kernel_two, bias_two), ("tile", "member")
+    kernel_one, bias_one, kernel_two, bias_two = perform_the_files(
+        (kernel_one, bias_one, kernel_two, bias_two)
     )
     return (
         response.reshape(fields.shape),

time: 489 us -> 1780 us (3.64); the launches traced: 479 us -> 1750 us
  waiting for transfers between devices: 255 us -> 1280 us
  blocking collectives: 73.3 us -> 320 us
    psum x1 -> x2, waiting for transfers between devices: 255 us -> 1280 us  [perform_the_files(): return psum(psum(arr, 'member'), 'tile')]
    psum x1 -> x2, blocking collectives: 73.3 us -> 320 us  [perform_the_files(): return psum(psum(arr, 'member'), 'tile')]
  transfers between devices with their start and end apart: 17 -> 18, of which waited for: 1 -> 1; matrix products, arithmetic and copies ran while one was open for 7% -> 2% of each run, Pallas kernels for 0% -> 0%
where the time goes in v1:
time: 1780 us; the launch traced here: 1750 us
  waiting for transfers between devices  1280 us (72%)
  blocking collectives  320 us (18%)
  local copies, waits for them, and re-layouts  56.4 us (3%)
  starting transfers between devices  41.2 us (2%)
  other arithmetic  18.3 us (1%)
    psum x2, waiting for transfers between devices, perform_the_files(): return psum(psum(arr, 'member'), 'tile')  1280 us
    psum x2, blocking collectives, perform_the_files(): return psum(psum(arr, 'member'), 'tile')  320 us
    ppermute x16, starting transfers between devices, shifted(): return lax.ppermute(value, axis, pairs)  41.1 us
  transfers between devices with their start and end apart: 18, of which 1 were waited for; matrix products, arithmetic and copies ran while one was open for 2% of the time, Pallas kernels for 0%

profile of v1, /device:TPU:2, one launch (start us, length us, event | category | flops | bytes accessed | tf_op | source)
XLA Modules:
  0.0 1750.4 jit_solution(9610941367719698346)
XLA Ops:
  10.2 1.6 collective-permute-start.3
  11.8 3.5 collective-permute-start.2
  15.3 6.0 collective-permute-start.1
  22.9 1.2 copy.158
  24.8 1.2 copy.140
  30.4 1.1 constant_dynamic-update-slice_fusion.3
  31.5 1.5 fusion.78
  33.5 1.4 fusion.84
  36.3 3.8 collective-permute-start.6
  40.0 6.2 collective-permute-start.5
  46.2 1.9 constant_dynamic-update-slice_fusion.18
  50.0 1.9 constant_dynamic-update-slice_fusion.15
  56.3 6.7 copy.180
  66.4 4.8 copy.182
  71.2 2.5 convert_reduce_fusion
  76.5 2.3 fusion.2
  80.7 6.7 copy.183
  93.7 1.4 select_select_fusion.3
  97.1 3.8 collective-permute-start.10
  100.8 6.0 collective-permute-start.9
  106.8 4.5 fusion.86
  111.5 1.1 copy.185
  117.4 2.1 fusion
  120.1 4.5 fusion.85
  125.0 3.8 collective-permute-start.14
  128.8 6.0 collective-permute-start.13
  134.8 5.1 all-reduce.4
  139.9 315.2 %all-reduce.2 = (f32[128]{0:T(128)S(1)}, f32[128]{0:T(128)S(1)}) all-reduce(f32[128]{0:T(128)S(1)} %get-tuple-element.316, f32[128]{0:T(128)S(1)} %get-tuple-element.317), channel_id=1, replica_groups=mesh['tile'=128,'member'=2] {'tile'}, use_global_device_ids=true, to_apply=%region_5.6 | all-reduce | flops 256 | bytes 2048 | tf_op jit(solution)/shard_map/psum | solution.py:185
  457.4 1.1 copy.186
  458.5 1280.8 %all-reduce.9.cloned.1.call-done = (f32[3,3,128,128]{3,2,1,0:T(8,128)}, f32[3,3,128,128]{3,2,1,0:T(8,128)}) async-done(((f32[3,3,128,128]{3,2,1,0:T(8,128)}, f32[3,3,128,128]{3,2,1,0:T(8,128)}), (f32[3,3,128,128]{3,2,1,0:T(8,128)}, f32[3,3,128,128]{3,2,1,0:T(8,128)})) %all-reduce.9.cloned.1.call-update) | async-done | bytes 1179664 | tf_op jit(solution)/shard_map/psum | solution.py:185
  1739.3 1.9 broadcast_multiply_fusion.1
  1741.3 1.9 broadcast_multiply_fusion
  (277 shorter events, 40.8 us)
Async XLA Ops:
  7.2 20.0 %copy-start = (bf16[1,1,2,32,32,128]{5,4,3,2,1,0:T(8,128)(2,1)S(1)}, bf16[1,1,2,32,32,128]{5,4,3,2,1,0:T(8,128)(2,1)}, u32[]{:S(2)}) copy-start(bf16[1,1,2,32,32,128]{5,4,3,2,1,0:T(8,128)(2,1)} %param.55) | copy-start | bytes 1572868
  7.2 449.5 %all-reduce.11.cloned.1.call-start = ((), (), s32[]{:S(2)}) async-start(), calls=%async_computation.1 | async-start | bytes 2359296 | tf_op jit(solution)/shard_map/psum | solution.py:185
  9.8 26.1 %copy-start.22 = (pred[4]{0:T(512)(128)(4,1)}, pred[4]{0:T(512)(128)(4,1)S(1)}, u32[]{:S(2)}) copy-start(pred[4]{0:T(512)(128)(4,1)S(1)} %get-tuple-element.431) | copy-start | bytes 16
  9.8 26.1 %copy-start.24 = (pred[4]{0:T(512)(128)(4,1)}, pred[4]{0:T(512)(128)(4,1)S(1)}, u32[]{:S(2)}) copy-start(pred[4]{0:T(512)(128)(4,1)S(1)} %get-tuple-element.432) | copy-start | bytes 16
  9.8 26.1 %copy-start.26 = (pred[4]{0:T(512)(128)(4,1)}, pred[4]{0:T(512)(128)(4,1)S(1)}, u32[]{:S(2)}) copy-start(pred[4]{0:T(512)(128)(4,1)S(1)} %get-tuple-element.433) | copy-start | bytes 16
  9.8 26.1 %copy-start.28 = (pred[4]{0:T(512)(128)(4,1)}, pred[4]{0:T(512)(128)(4,1)S(1)}, u32[]{:S(2)}) copy-start(pred[4]{0:T(512)(128)(4,1)S(1)} %get-tuple-element.434) | copy-start | bytes 16
  9.8 26.1 %copy-start.32 = (pred[4]{0:T(512)(128)(4,1)}, pred[4]{0:T(512)(128)(4,1)S(1)}, u32[]{:S(2)}) copy-start(pred[4]{0:T(512)(128)(4,1)S(1)} %get-tuple-element.430) | copy-start | bytes 16
  10.1 16.6 collective-permute-start
  10.2 16.5 collective-permute-start.3
  11.8 15.0 collective-permute-start.2
  15.3 11.5 collective-permute-start.1
  22.8 40.4 %copy-start.14 = (pred[4]{0:T(512)(128)(4,1)}, pred[4]{0:T(512)(128)(4,1)S(1)}, u32[]{:S(2)}) copy-start(pred[4]{0:T(512)(128)(4,1)S(1)} %get-tuple-element.436) | copy-start | bytes 16
  22.8 40.4 %copy-start.16 = (pred[4]{0:T(512)(128)(4,1)}, pred[4]{0:T(512)(128)(4,1)S(1)}, u32[]{:S(2)}) copy-start(pred[4]{0:T(512)(128)(4,1)S(1)} %get-tuple-element.437) | copy-start | bytes 16
  22.9 40.4 %copy-start.18 = (pred[4]{0:T(512)(128)(4,1)}, pred[4]{0:T(512)(128)(4,1)S(1)}, u32[]{:S(2)}) copy-start(pred[4]{0:T(512)(128)(4,1)S(1)} %get-tuple-element.438) | copy-start | bytes 16
  22.9 40.4 %copy-start.20 = (pred[4]{0:T(512)(128)(4,1)}, pred[4]{0:T(512)(128)(4,1)S(1)}, u32[]{:S(2)}) copy-start(pred[4]{0:T(512)(128)(4,1)S(1)} %get-tuple-element.439) | copy-start | bytes 16
  22.9 40.4 %copy-start.30 = (pred[4]{0:T(512)(128)(4,1)}, pred[4]{0:T(512)(128)(4,1)S(1)}, u32[]{:S(2)}) copy-start(pred[4]{0:T(512)(128)(4,1)S(1)} %get-tuple-element.435) | copy-start | bytes 16
  36.0 17.7 %copy-start.4 = (bf16[2,32,32,128]{3,2,1,0:T(8,128)(2,1)S(1)}, bf16[2,32,32,128]{3,2,1,0:T(8,128)(2,1)}, u32[]{:S(2)}) copy-start(bf16[2,32,32,128]{3,2,1,0:T(8,128)(2,1)} %get-tuple-element.357) | copy-start | bytes 1572868
  36.0 18.5 %copy-start.3 = (bf16[2,32,32,128]{3,2,1,0:T(8,128)(2,1)S(1)}, bf16[2,32,32,128]{3,2,1,0:T(8,128)(2,1)}, u32[]{:S(2)}) copy-start(bf16[2,32,32,128]{3,2,1,0:T(8,128)(2,1)} %get-tuple-element.356) | copy-start | bytes 1572868
  36.0 19.5 %copy-start.1 = (bf16[2,32,32,128]{3,2,1,0:T(8,128)(2,1)S(1)}, bf16[2,32,32,128]{3,2,1,0:T(8,128)(2,1)}, u32[]{:S(2)}) copy-start(bf16[2,32,32,128]{3,2,1,0:T(8,128)(2,1)} %get-tuple-element.354) | copy-start | bytes 1572868
  36.1 27.0 %collective-permute-start.4 = (bf16[2,32,128]{2,1,0:T(8,128)(2,1)S(1)}, bf16[2,32,128]{2,1,0:T(8,128)(2,1)S(1)}, u32[]{:S(2)}, u32[]{:S(2)}) collective-permute-start(bf16[2,32,128]{2,1,0:T(8,128)(2,1)S(1)} %get-tuple-element.392), channel_id=1, source_target_pairs={{0,2},{2,4},{4,6},{6,8},{8,10},{10,12},{12,14},{14,16},{16,18},{18... | collective-permute-start | bytes 49160 | tf_op jit(solution)/shard_map/ppermute | solution.py:15
  36.2 26.9 %collective-permute-start.7 = (bf16[2,32,128]{2,1,0:T(8,128)(2,1)S(1)}, bf16[2,32,128]{2,1,0:T(8,128)(2,1)S(1)}, u32[]{:S(2)}, u32[]{:S(2)}) collective-permute-start(bf16[2,32,128]{2,1,0:T(8,128)(2,1)S(1)} %get-tuple-element.393), channel_id=1, source_target_pairs={{0,16},{2,18},{4,20},{6,22},{8,24},{10,26},{12,28},{14,30},{16,32}... | collective-permute-start | bytes 49160 | tf_op jit(solution)/shard_map/ppermute | solution.py:15
  36.3 26.8 %collective-permute-start.6 = (bf16[2,32,128]{2,1,0:T(8,128)(2,1)S(1)}, bf16[2,32,128]{2,1,0:T(8,128)(2,1)S(1)}, u32[]{:S(2)}, u32[]{:S(2)}) collective-permute-start(bf16[2,32,128]{2,1,0:T(8,128)(2,1)S(1)} %get-tuple-element.394), channel_id=1, source_target_pairs={{0,254},{2,0},{4,2},{6,4},{8,6},{10,8},{12,10},{14,12},{16,14},{18... | collective-permute-start | bytes 49160 | tf_op jit(solution)/shard_map/ppermute | solution.py:15
  40.0 23.0 %collective-permute-start.5 = (bf16[2,32,128]{2,1,0:T(8,128)(2,1)S(1)}, bf16[2,32,128]{2,1,0:T(8,128)(2,1)S(1)}, u32[]{:S(2)}, u32[]{:S(2)}) collective-permute-start(bf16[2,32,128]{2,1,0:T(8,128)(2,1)S(1)} %get-tuple-element.395), channel_id=1, source_target_pairs={{0,240},{2,242},{4,244},{6,246},{8,248},{10,250},{12,252},{14,254}... | collective-permute-start | bytes 49160 | tf_op jit(solution)/shard_map/ppermute | solution.py:15
  96.9 15.9 collective-permute-start.8
  97.0 15.8 collective-permute-start.11
  97.1 15.8 collective-permute-start.10
  100.8 12.0 collective-permute-start.9
  124.7 1614.7 %all-reduce.9.cloned.1.call-start = ((), (), s32[]{:S(2)}) async-start(), calls=%async_computation | async-start | bytes 2359296 | tf_op jit(solution)/shard_map/psum | solution.py:185
  124.9 331.5 %collective-permute-start.12 = (bf16[2,32,128]{2,1,0:T(8,128)(2,1)S(1)}, bf16[2,32,128]{2,1,0:T(8,128)(2,1)S(1)}, u32[]{:S(2)}, u32[]{:S(2)}) collective-permute-start(bf16[2,32,128]{2,1,0:T(8,128)(2,1)S(1)} %get-tuple-element.378), channel_id=1, source_target_pairs={{0,2},{2,4},{4,6},{6,8},{8,10},{10,12},{12,14},{14,16},{16,18},{18... | collective-permute-start | bytes 49160 | tf_op jit(solution)/shard_map/ppermute | solution.py:15
  124.9 331.4 %collective-permute-start.15 = (bf16[2,32,128]{2,1,0:T(8,128)(2,1)S(1)}, bf16[2,32,128]{2,1,0:T(8,128)(2,1)S(1)}, u32[]{:S(2)}, u32[]{:S(2)}) collective-permute-start(bf16[2,32,128]{2,1,0:T(8,128)(2,1)S(1)} %get-tuple-element.379), channel_id=1, source_target_pairs={{0,16},{2,18},{4,20},{6,22},{8,24},{10,26},{12,28},{14,30},{16,32}... | collective-permute-start | bytes 49160 | tf_op jit(solution)/shard_map/ppermute | solution.py:15
  125.0 331.3 %collective-permute-start.14 = (bf16[2,32,128]{2,1,0:T(8,128)(2,1)S(1)}, bf16[2,32,128]{2,1,0:T(8,128)(2,1)S(1)}, u32[]{:S(2)}, u32[]{:S(2)}) collective-permute-start(bf16[2,32,128]{2,1,0:T(8,128)(2,1)S(1)} %get-tuple-element.380), channel_id=1, source_target_pairs={{0,254},{2,0},{4,2},{6,4},{8,6},{10,8},{12,10},{14,12},{16,14},{18... | collective-permute-start | bytes 49160 | tf_op jit(solution)/shard_map/ppermute | solution.py:15
  128.8 327.6 %collective-permute-start.13 = (bf16[2,32,128]{2,1,0:T(8,128)(2,1)S(1)}, bf16[2,32,128]{2,1,0:T(8,128)(2,1)S(1)}, u32[]{:S(2)}, u32[]{:S(2)}) collective-permute-start(bf16[2,32,128]{2,1,0:T(8,128)(2,1)S(1)} %get-tuple-element.381), channel_id=1, source_target_pairs={{0,240},{2,242},{4,244},{6,246},{8,248},{10,250},{12,252},{14,254}... | collective-permute-start | bytes 49160 | tf_op jit(solution)/shard_map/ppermute | solution.py:15
  (27 other events, 114.3 us)
Sparse Core Ops, SparseCore 0:
  124.8 51.7 all-reduce.10
  456.8 1282.4 all-reduce.8
